TPU v7x, 32 devices: a whole 2x2x4 slice. The times are simulated.
32 devices in a mesh: lev: 4 (over x, core), gy: 8 (over z, y).
Axes of the slice: x: 2, y: 2, z: 4, core: 2. Of those that a mesh axis runs over, the one named last changes fastest.
Arguments:
- forcing: bfloat16 [4, 32, 768, 1024], P('lev', None, 'gy'), may hold values from -6 to 6
- spectral_weight: bfloat16 [2, 128, 32, 32, 128], P(None, 'gy'), may hold values from -4.1875 to 4.1875
- point_weight: bfloat16 [32, 32], replicated, may hold values from -1 to 1
- point_bias: float32 [32], replicated, may hold values from -3 to 3
- decoder: bfloat16 [4, 32], replicated, may hold values from -1 to 1
- coriolis: float32 [768], P('gy'), may hold values from -1.5 to 1.5
- layer_depth: float32 [4], replicated, may hold values from 0.5 to 2
Outputs:
- equilibrium: float32 [4, 32, 768, 1024], P('lev', None, 'gy')
- residual: float32 [3, 4, 768, 1024], P(None, 'lev', 'gy')
All inputs are finite; a program needn't handle non-finite values.
Results may differ from a plain program's by a relative error of at most 0.015.
Values may be sent and summed in bfloat16 or wider, within the bound.
No kernel may reach another device: no remote copies, remote signals or barrier semaphores. Data moves between devices by JAX's collectives and lax.ppermute only.
A program may use at most 128 MiB of HBM per device.

v0:
```python
import math
import jax
import jax.numpy as jnp
from jax import lax
from jax.sharding import PartitionSpec as P

ITERS = 3


def prefix(value, axis, combine, identity):
    peers, place = (lax.axis_size(axis), lax.axis_index(axis))
    everything = lax.all_gather(value, axis)
    start = jnp.broadcast_to(jnp.asarray(identity, value.dtype), value.shape)

    def hop(k, before):
        reached = k < place
        new = combine(before, everything[k])
        return jnp.where(reached, new, before)

    return lax.fori_loop(0, peers, hop, start)


def from_behind(value, axis, steps):
    count = lax.axis_size(axis)
    initial, last = (max(0, -steps), min(count, count - steps))
    return lax.ppermute(value, axis, [(source, source + steps) for source in range(initial, last)])


def extended(value, sides, width):
    for axis, dim in sides:
        peers, length = (lax.axis_size(axis), value.shape[dim])
        up = [(i, (i + 1) % peers) for i in range(peers)]
        down = [(j, i) for i, j in up]
        last = lax.slice_in_dim(value, length - width, length, axis=dim)
        initial = lax.slice_in_dim(value, 0, width, axis=dim)
        before = lax.ppermute(last, axis, up)
        after = lax.ppermute(initial, axis, down)
        value = jnp.concatenate([before, value, after], axis=dim)
    return value


def angles(row_index, col_index, length):
    phase = row_index[:, None] * col_index[None, :] % length
    return phase.astype(jnp.float32) * (2.0 * math.pi / length)


def signed_modes(length, count):
    index = jnp.arange(count, dtype=jnp.int32)
    return jnp.where(index < count // 2, index, index + (length - count))


def forward_x(length, count):
    turned = angles(jnp.arange(length, dtype=jnp.int32), jnp.arange(count, dtype=jnp.int32), length)
    return jnp.stack([jnp.cos(turned), -jnp.sin(turned)], 0).astype(jnp.bfloat16)


def forward_y(row_index, length, count):
    turned = angles(row_index, signed_modes(length, count), length)
    cosine = jnp.cos(turned)
    sine = jnp.sin(turned)
    return jnp.stack([jnp.stack([cosine, -sine], 1), jnp.stack([sine, cosine], 1)], 0).astype(
        jnp.bfloat16
    )


def inverse_y(row_index, length, count):
    turned = angles(signed_modes(length, count), row_index, length)
    cosine = jnp.cos(turned)
    sine = jnp.sin(turned)
    return jnp.stack([jnp.stack([cosine, sine], 1), jnp.stack([-sine, cosine], 1)], 0).astype(
        jnp.bfloat16
    )


def inverse_x(length, count, total):
    index = jnp.arange(count, dtype=jnp.int32)
    turned = angles(index, jnp.arange(length, dtype=jnp.int32), length)
    factor = jnp.where(index == 0, 1.0, 2.0).astype(jnp.float32)[:, None] / total
    return jnp.stack([factor * jnp.cos(turned), -factor * jnp.sin(turned)], 0).astype(jnp.bfloat16)


def mix_modes(spectrum, weights):
    real_part = spectrum[:, :, 0]
    imag_part = spectrum[:, :, 1]
    weight_real = weights[0].astype(jnp.float32)
    weight_imag = weights[1].astype(jnp.float32)
    highest = lax.Precision.HIGHEST
    out_real = jnp.einsum(
        "klim,kiom->klom", real_part, weight_real, precision=highest
    ) - jnp.einsum("klim,kiom->klom", imag_part, weight_imag, precision=highest)
    out_imag = jnp.einsum(
        "klim,kiom->klom", real_part, weight_imag, precision=highest
    ) + jnp.einsum("klim,kiom->klom", imag_part, weight_real, precision=highest)
    return jnp.stack([out_real, out_imag], 2).astype(jnp.bfloat16)


def add_terms(earlier, later):
    return earlier + later


def roll_diff(field, axis):
    return (jnp.roll(field, -1, axis) - jnp.roll(field, 1, axis)) * 0.5


def on_device(forcing, spectral_weight, point_weight, point_bias, decoder, coriolis, layer_depth):
    level_count, channels, row_count, cell_count = forcing.shape
    group_size = lax.axis_size("gy")
    total_rows = row_count * group_size
    own_mode_count = spectral_weight.shape[1]
    mode_count = own_mode_count * group_size
    ymode_count = spectral_weight.shape[4]
    every_row = jnp.arange(total_rows, dtype=jnp.int32)
    table_fx = forward_x(cell_count, mode_count)
    table_ix = inverse_x(cell_count, mode_count, cell_count * total_rows)
    source = forcing.astype(jnp.float32) + point_bias[None, :, None, None]
    current = forcing
    updated = source
    for iteration in range(ITERS):
        near_modes = jnp.einsum(
            "lcyx,rxk->lrcky", current, table_fx, preferred_element_type=jnp.float32
        ).astype(jnp.bfloat16)
        all_rows = lax.all_to_all(near_modes, "gy", split_axis=3, concat_axis=4, tiled=True)
        table_fy = forward_y(every_row, total_rows, ymode_count)
        spectrum = jnp.einsum(
            "lrcky,ryqm->klqcm", all_rows, table_fy, preferred_element_type=jnp.float32
        )
        mixed = mix_modes(spectrum, spectral_weight)
        table_iy = inverse_y(every_row, total_rows, ymode_count)
        back_rows = jnp.einsum(
            "klqcm,qmry->lrcky", mixed, table_iy, preferred_element_type=jnp.float32
        ).astype(jnp.bfloat16)
        own_modes = lax.all_to_all(back_rows, "gy", split_axis=4, concat_axis=3, tiled=True)
        spread = jnp.einsum(
            "lrcky,rkx->lcyx", own_modes, table_ix, preferred_element_type=jnp.float32
        )
        pointwise = jnp.einsum(
            "lcyx,co->loyx", current, point_weight, preferred_element_type=jnp.float32
        )
        updated = jax.nn.gelu(spread + pointwise + source, approximate=True)
        current = updated.astype(jnp.bfloat16)
    fields = jnp.einsum(
        "lcyx,fc->flyx", updated, decoder.astype(jnp.float32), precision=lax.Precision.HIGHEST
    )
    turning = coriolis[:, None]
    east_wind = fields[0]
    north_wind = fields[1]
    upward = fields[2]
    heat = fields[3]
    level_start = lax.axis_index("lev") * level_count
    own_depth = lax.dynamic_slice_in_dim(layer_depth, level_start, level_count, 0)
    inside = jnp.cumsum(own_depth[:, None, None] * heat, axis=0)
    lower_sum = prefix(inside[-1], "lev", add_terms, jnp.zeros_like(inside[-1]))
    geopotential = inside + lower_sum[None]
    lower_wind = from_behind(upward[-1], "lev", 1)
    below_level = jnp.concatenate([lower_wind[None], upward[:-1]], 0)
    rimmed = extended(jnp.stack([north_wind, geopotential], 0), (("gy", 2),), 1)
    along_y = (rimmed[:, :, 2:, :] - rimmed[:, :, :-2, :]) * 0.5
    continuity = roll_diff(east_wind, 2) + along_y[0] + upward - below_level
    balance_x = turning * north_wind - roll_diff(geopotential, 2)
    balance_y = turning * east_wind + along_y[1]
    residual = jnp.stack([continuity, balance_x, balance_y], 0)
    return (updated, residual)


def solution(mesh):
    return jax.shard_map(
        on_device,
        mesh=mesh,
        in_specs=(
            P("lev", None, "gy", None),
            P(None, "gy", None, None, None),
            P(),
            P(),
            P(),
            P("gy"),
            P(),
        ),
        out_specs=(P("lev", None, "gy", None), P(None, "lev", "gy", None)),
        check_vma=False,
    )
```

profile of v0, /device:TPU:1, one launch (start us, length us, event | category | flops | bytes accessed | tf_op | source)
XLA Modules:
  0.0 566.0 jit_solution(12187804742954895769)
XLA Ops:
  9.4 4.7 fusion.67
  14.1 2.9 copy.119
  17.0 6.6 %all-to-all-start = ((bf16[1,2,32,128,96]{4,2,1,0,3:T(8,128)(2,1)}), bf16[1,2,32,128,96]{4,2,1,0,3:T(8,128)(2,1)S(1)}, u32[]{:S(2)}, u32[]{:S(2)}) async-start(bf16[1,2,32,128,96]{4,2,1,0,3:T(8,128)(2,1)} %copy.119), calls=%async_computation | async-start | bytes 4194304 | tf_op jit(solution)/shard_map/all_to_all | solution.py:122
  28.0 42.9 %all-to-all-done = bf16[1,2,32,128,96]{4,2,1,0,3:T(8,128)(2,1)S(1)} async-done(((bf16[1,2,32,128,96]{4,2,1,0,3:T(8,128)(2,1)}), bf16[1,2,32,128,96]{4,2,1,0,3:T(8,128)(2,1)S(1)}, u32[]{:S(2)}, u32[]{:S(2)}) %all-to-all-start) | async-done | bytes 1572896 | tf_op jit(solution)/shard_map/all_to_all | solution.py:122
  72.8 2.7 reshape.706
  77.7 5.1 fusion.31
  83.5 9.2 %copy.122 = bf16[1,2,32,16,768]{2,3,1,0,4:T(8,128)(2,1)} copy(bf16[1,2,32,16,768]{4,2,3,1,0:T(8,128)(2,1)S(1)} %fusion.58) | data formatting | bytes 3145728 | tf_op jit(solution)/shard_map/convert_element_type | solution.py:131
  92.6 9.5 %reshape.756 = bf16[8,2,49152]{2,1,0:T(2,128)(2,1)} reshape(bf16[768,1,2,16,32]{4,3,2,1,0:T(8,128)(2,1)} %bitcast.368) | data formatting | bytes 3145728
  102.1 4.9 all-to-all-start.1
  107.0 3.0 multiply_convert_fusion
  110.0 16.3 %fusion.47 = f32[32,96,1024]{2,0,1:T(8,128)} fusion(bf16[32,96,1024]{2,1,0:T(8,128)(2,1)} %bitcast.383, bf16[32,32]{1,0:T(8,128)(2,1)S(1)} %copy-done), kind=kOutput, calls=%fused_computation.70 | convolution fusion | flops 201326592 | bytes 18876416 | tf_op jit(solution)/shard_map/lcyx,co->loyx/dot_general | solution.py:136
  126.3 17.0 %all-to-all-done.1 = bf16[8,2,49152]{2,1,0:T(2,128)(2,1)S(1)} async-done(((bf16[8,2,49152]{2,1,0:T(2,128)(2,1)}), bf16[8,2,49152]{2,1,0:T(2,128)(2,1)S(1)}, u32[]{:S(2)}, u32[]{:S(2)}) %all-to-all-start.1) | async-done | bytes 1572896 | tf_op jit(solution)/shard_map/all_to_all | solution.py:132
  143.3 5.3 reshape.757
  148.7 8.5 %copy.123 = bf16[1,2,32,16,8,96]{5,3,4,2,1,0:T(8,128)(2,1)S(1)} copy(bf16[1,2,32,16,8,96]{2,3,1,5,4,0:T(8,128)(2,1)} %bitcast.369) | data formatting | bytes 3145728 | tf_op jit(solution)/shard_map/all_to_all | solution.py:132
  157.2 16.4 %fusion.7 = bf16[1,32,96,1024]{3,2,1,0:T(8,128)(2,1)S(1)} fusion(f32[32,96,1024]{2,0,1:T(8,128)} %fusion.47, bf16[1,32,96,1024]{3,2,1,0:T(8,128)(2,1)} %param.9, f32[32]{0:T(128)S(1)} %copy-done.13, bf16[2,32,128,96]{3,2,1,0:T(8,128)(2,1)S(1)} %bitcast.387, bf16[1,128,1024]{2,1,0:T(8,128)(2,1)} %get-tuple-element.164, ...), kind=kOutput, calls=%fused_computation.23 | convolution fusion | flops 1651769344 | bytes 27263104 | tf_op jit(solution)/shard_map/lrcky,rkx->lcyx/dot_general | solution.py:133
  176.3 2.9 fusion.64
  179.3 3.4 copy.128
  182.7 51.9 %all_to_all.90 = bf16[1,2,32,128,96]{4,2,1,0,3:T(8,128)(2,1)S(1)} all-to-all(bf16[1,2,32,128,96]{4,2,1,0,3:T(8,128)(2,1)S(1)} %copy.128), channel_id=1, replica_groups=mesh['lev'=4,'gy'=8] {'gy'}, dimensions={3} | all-to-all | bytes 3145728 | tf_op jit(solution)/shard_map/all_to_all | solution.py:122
  236.5 2.7 reshape.723
  241.3 5.1 fusion.33
  247.1 9.2 %copy.131 = bf16[1,2,32,16,768]{2,3,1,0,4:T(8,128)(2,1)} copy(bf16[1,2,32,16,768]{4,2,3,1,0:T(8,128)(2,1)S(1)} %fusion.59) | data formatting | bytes 3145728 | tf_op jit(solution)/shard_map/convert_element_type | solution.py:131
  256.3 9.5 %reshape.758 = bf16[8,2,49152]{2,1,0:T(2,128)(2,1)} reshape(bf16[768,1,2,16,32]{4,3,2,1,0:T(8,128)(2,1)} %bitcast.370) | data formatting | bytes 3145728
  265.8 4.4 all-to-all-start.3
  270.3 11.6 %fusion.45 = f32[96,1024,32]{1,2,0:T(8,128)} fusion(bf16[32,96,1024]{2,1,0:T(8,128)(2,1)} %bitcast.385, bf16[32,32]{1,0:T(8,128)(2,1)S(1)} %copy-done), kind=kOutput, calls=%fused_computation.68 | convolution fusion | flops 201326592 | bytes 18876416 | tf_op jit(solution)/shard_map/lcyx,co->loyx/dot_general | solution.py:136
  281.9 24.2 %all-to-all-done.3 = bf16[8,2,49152]{2,1,0:T(2,128)(2,1)S(1)} async-done(((bf16[8,2,49152]{2,1,0:T(2,128)(2,1)}), bf16[8,2,49152]{2,1,0:T(2,128)(2,1)S(1)}, u32[]{:S(2)}, u32[]{:S(2)}) %all-to-all-start.3) | async-done | bytes 1572896 | tf_op jit(solution)/shard_map/all_to_all | solution.py:132
  306.0 5.3 reshape.759
  311.4 8.5 %copy.132 = bf16[1,2,32,16,8,96]{5,3,4,2,1,0:T(8,128)(2,1)S(1)} copy(bf16[1,2,32,16,8,96]{2,3,1,5,4,0:T(8,128)(2,1)} %bitcast.371) | data formatting | bytes 3145728 | tf_op jit(solution)/shard_map/all_to_all | solution.py:132
  319.9 16.4 %fusion.15 = bf16[1,32,96,1024]{3,2,1,0:T(8,128)(2,1)S(1)} fusion(f32[96,1024,32]{1,2,0:T(8,128)} %fusion.45, bf16[1,32,96,1024]{3,2,1,0:T(8,128)(2,1)} %param.9, f32[32]{0:T(128)S(1)} %copy-done.13, bf16[2,32,128,96]{3,2,1,0:T(8,128)(2,1)S(1)} %bitcast.388, bf16[1,128,1024]{2,1,0:T(8,128)(2,1)} %get-tuple-element.164, ...), kind=kOutput, calls=%fused_computation.31 | convolution fusion | flops 1651769344 | bytes 27263104 | tf_op jit(solution)/shard_map/lrcky,rkx->lcyx/dot_general | solution.py:133
  339.0 2.9 fusion.61
  341.9 3.4 copy.137
  345.3 52.0 %all_to_all.91 = bf16[1,2,32,128,96]{4,2,1,0,3:T(8,128)(2,1)S(1)} all-to-all(bf16[1,2,32,128,96]{4,2,1,0,3:T(8,128)(2,1)S(1)} %copy.137), channel_id=1, replica_groups=mesh['lev'=4,'gy'=8] {'gy'}, dimensions={3} | all-to-all | bytes 3145728 | tf_op jit(solution)/shard_map/all_to_all | solution.py:122
  399.3 2.7 reshape.738
  404.1 5.1 fusion.35
  409.9 9.2 %copy.140 = bf16[1,2,32,16,768]{2,3,1,0,4:T(8,128)(2,1)} copy(bf16[1,2,32,16,768]{4,2,3,1,0:T(8,128)(2,1)S(1)} %fusion.60) | data formatting | bytes 3145728 | tf_op jit(solution)/shard_map/convert_element_type | solution.py:131
  419.1 9.5 %reshape.760 = bf16[8,2,49152]{2,1,0:T(2,128)(2,1)} reshape(bf16[768,1,2,16,32]{4,3,2,1,0:T(8,128)(2,1)} %bitcast.372) | data formatting | bytes 3145728
  428.6 4.2 all-to-all-start.5
  433.9 11.6 %fusion.43 = f32[96,1024,32]{1,2,0:T(8,128)} fusion(bf16[32,96,1024]{2,1,0:T(8,128)(2,1)} %bitcast.384, bf16[32,32]{1,0:T(8,128)(2,1)S(1)} %copy-done), kind=kOutput, calls=%fused_computation.66 | convolution fusion | flops 201326592 | bytes 18876416 | tf_op jit(solution)/shard_map/lcyx,co->loyx/dot_general | solution.py:136
  445.5 23.2 %all-to-all-done.5 = bf16[8,2,49152]{2,1,0:T(2,128)(2,1)S(1)} async-done(((bf16[8,2,49152]{2,1,0:T(2,128)(2,1)}), bf16[8,2,49152]{2,1,0:T(2,128)(2,1)S(1)}, u32[]{:S(2)}, u32[]{:S(2)}) %all-to-all-start.5) | async-done | bytes 1572896 | tf_op jit(solution)/shard_map/all_to_all | solution.py:132
  468.7 5.3 reshape.761
  474.0 8.5 %copy.141 = bf16[1,2,32,16,8,96]{5,3,4,2,1,0:T(8,128)(2,1)S(1)} copy(bf16[1,2,32,16,8,96]{2,3,1,5,4,0:T(8,128)(2,1)} %bitcast.373) | data formatting | bytes 3145728 | tf_op jit(solution)/shard_map/all_to_all | solution.py:132
  482.6 17.6 %fusion.22 = f32[1,32,96,1024]{3,2,1,0:T(8,128)S(1)} fusion(f32[96,1024,32]{1,2,0:T(8,128)} %fusion.43, bf16[1,32,96,1024]{3,2,1,0:T(8,128)(2,1)} %param.9, f32[32]{0:T(128)S(1)} %copy-done.13, bf16[2,32,128,96]{3,2,1,0:T(8,128)(2,1)S(1)} %bitcast.386, bf16[1,128,1024]{2,1,0:T(8,128)(2,1)S(1)} %copy-done.8, bf16[1,128,1024]{2,1,0:T(8,128)(2,1)S(1)} %copy-done.9), kind=kOutput, calls=%fused_computation.38 | convolution fusion | flops 1648623616 | bytes 33554560 | tf_op jit(solution)/shard_map/lrcky,rkx->lcyx/dot_general | solution.py:133
  500.2 11.3 %fusion.23 = f32[96,1024,4]{1,2,0:T(4,128)S(1)} fusion(f32[32,96,1024]{2,1,0:T(8,128)S(1)} %bitcast.379, bf16[4,32]{1,0:T(4,128)(2,1)S(1)} %copy-done.10), kind=kOutput, calls=%fused_computation.45 | convolution fusion | flops 150994944 | bytes 14156032 | tf_op jit(solution)/shard_map/lcyx,fc->flyx/dot_general | solution.py:141
  514.0 20.7 %all-gather.2.cloned.1.call-done = f32[4,96,1024]{2,1,0:T(8,128)} async-done(((f32[1,96,1024]{2,1,0:T(8,128)}), f32[4,96,1024]{2,1,0:T(8,128)}) %all-gather.2.cloned.1.call-update) | async-done | bytes 1572880 | tf_op jit(solution)/shard_map/all_gather | solution.py:12
  534.7 4.6 while.14
  539.5 4.0 collective-permute-start
  544.3 4.4 collective-permute-done.1
  549.1 3.8 collective-permute-start.2
  553.2 4.4 collective-permute-done.2
  (79 shorter events, 37.1 us)
Async XLA Ops:
  7.2 102.8 %copy-start = (bf16[32,32]{1,0:T(8,128)(2,1)S(1)}, bf16[32,32]{1,0:T(8,128)(2,1)}, u32[]{:S(2)}) copy-start(bf16[32,32]{1,0:T(8,128)(2,1)} %param.11) | copy-start | bytes 6148
  9.4 4.7 copy-start.5
  17.0 54.0 %all-to-all-start = ((bf16[1,2,32,128,96]{4,2,1,0,3:T(8,128)(2,1)}), bf16[1,2,32,128,96]{4,2,1,0,3:T(8,128)(2,1)S(1)}, u32[]{:S(2)}, u32[]{:S(2)}) async-start(bf16[1,2,32,128,96]{4,2,1,0,3:T(8,128)(2,1)} %copy.119), calls=%async_computation | async-start | bytes 4194304 | tf_op jit(solution)/shard_map/all_to_all | solution.py:122
  102.1 41.2 %all-to-all-start.1 = ((bf16[8,2,49152]{2,1,0:T(2,128)(2,1)}), bf16[8,2,49152]{2,1,0:T(2,128)(2,1)S(1)}, u32[]{:S(2)}, u32[]{:S(2)}) async-start(bf16[8,2,49152]{2,1,0:T(2,128)(2,1)} %reshape.756), calls=%async_computation.1 | async-start | bytes 3145728 | tf_op jit(solution)/shard_map/all_to_all | solution.py:132
  126.3 30.9 %copy-start.13 = (f32[32]{0:T(128)S(1)}, f32[32]{0:T(128)}, u32[]{:S(2)}) copy-start(f32[32]{0:T(128)} %param.12) | copy-start | bytes 388
  157.2 19.1 %copy-start.6 = (bf16[1,1024,128]{2,1,0:T(8,128)(2,1)S(1)}, bf16[1,1024,128]{2,1,0:T(8,128)(2,1)}, u32[]{:S(2)}) copy-start(bf16[1,1024,128]{2,1,0:T(8,128)(2,1)} %copy-done.5) | copy-start | bytes 786436
  173.7 2.6 copy-start.3
  265.8 40.2 %all-to-all-start.3 = ((bf16[8,2,49152]{2,1,0:T(2,128)(2,1)}), bf16[8,2,49152]{2,1,0:T(2,128)(2,1)S(1)}, u32[]{:S(2)}, u32[]{:S(2)}) async-start(bf16[8,2,49152]{2,1,0:T(2,128)(2,1)} %reshape.758), calls=%async_computation.3 | async-start | bytes 3145728 | tf_op jit(solution)/shard_map/all_to_all | solution.py:132
  319.9 19.1 %copy-start.7 = (bf16[1,1024,128]{2,1,0:T(8,128)(2,1)S(1)}, bf16[1,1024,128]{2,1,0:T(8,128)(2,1)}, u32[]{:S(2)}) copy-start(bf16[1,1024,128]{2,1,0:T(8,128)(2,1)} %copy-done.5) | copy-start | bytes 786436
  336.3 2.6 copy-start.2
  419.1 14.2 %copy-start.12 = (f32[4]{0:T(128)S(1)}, f32[4]{0:T(128)}, u32[]{:S(2)}) copy-start(f32[4]{0:T(128)} %param.15) | copy-start | bytes 52
  428.6 40.1 %all-to-all-start.5 = ((bf16[8,2,49152]{2,1,0:T(2,128)(2,1)}), bf16[8,2,49152]{2,1,0:T(2,128)(2,1)S(1)}, u32[]{:S(2)}, u32[]{:S(2)}) async-start(bf16[8,2,49152]{2,1,0:T(2,128)(2,1)} %reshape.760), calls=%async_computation.5 | async-start | bytes 3145728 | tf_op jit(solution)/shard_map/all_to_all | solution.py:132
  432.8 101.9 %all-gather.2.cloned.1.call-start = ((), (), s32[]{:S(2)}) async-start(), calls=%async_computation.6 | async-start | bytes 1966080 | tf_op jit(solution)/shard_map/all_gather | solution.py:12
  445.5 37.0 %copy-start.8 = (bf16[1,128,1024]{2,1,0:T(8,128)(2,1)S(1)}, bf16[1,128,1024]{2,1,0:T(8,128)(2,1)}, u32[]{:S(2)}) copy-start(bf16[1,128,1024]{2,1,0:T(8,128)(2,1)} %get-tuple-element.164) | copy-start | bytes 786436
  445.5 37.0 %copy-start.9 = (bf16[1,128,1024]{2,1,0:T(8,128)(2,1)S(1)}, bf16[1,128,1024]{2,1,0:T(8,128)(2,1)}, u32[]{:S(2)}) copy-start(bf16[1,128,1024]{2,1,0:T(8,128)(2,1)} %get-tuple-element.165) | copy-start | bytes 786436
  482.5 17.6 %copy-start.10 = (bf16[4,32]{1,0:T(4,128)(2,1)S(1)}, bf16[4,32]{1,0:T(4,128)(2,1)}, u32[]{:S(2)}) copy-start(bf16[4,32]{1,0:T(4,128)(2,1)} %param.13) | copy-start | bytes 772
  500.2 11.3 %copy-start.1 = (f32[1,32,96,1024]{3,2,1,0:T(8,128)}, f32[1,32,96,1024]{3,2,1,0:T(8,128)S(1)}, u32[]{:S(2)}) copy-start(f32[1,32,96,1024]{3,2,1,0:T(8,128)S(1)} %fusion.22) | copy-start | bytes 37748740
  514.0 25.3 %copy-start.4 = (f32[1,96,1024]{2,1,0:T(8,128)S(1)}, f32[1,96,1024]{2,1,0:T(8,128)}, u32[]{:S(2)}) copy-start(f32[1,96,1024]{2,1,0:T(8,128)} %get-tuple-element.137) | copy-start | bytes 1179652
  514.0 34.8 %copy-start.11 = (f32[96]{0:T(128)S(1)}, f32[96]{0:T(128)}, u32[]{:S(2)}) copy-start(f32[96]{0:T(128)} %param.14) | copy-start | bytes 1156
  539.5 4.8 collective-permute-start
  543.5 5.2 collective-permute-start.1
  549.1 8.5 %collective-permute-start.2 = (f32[96,1024]{1,0:T(8,128)S(1)}, f32[96,1024]{1,0:T(8,128)S(1)}, u32[]{:S(2)}, u32[]{:S(2)}) collective-permute-start(f32[96,1024]{1,0:T(8,128)S(1)} %get-tuple-element.135), channel_id=1, source_target_pairs={{0,8},{8,16},{16,24},{1,9},{9,17},{17,25},{2,10},{10,18},{18,26},{... | collective-permute-start | bytes 1179656 | tf_op jit(solution)/shard_map/ppermute | solution.py:26
Sparse Core Ops, SparseCore 0:
  514.2 20.5 all-gather.1
where the time goes:
time: 571 us; the launch traced here: 566 us
  waiting for transfers between devices  137 us (24%)
  local copies, waits for them, and re-layouts  129 us (23%)
  matrix products  120 us (21%)
  blocking collectives  104 us (18%)
  other arithmetic  32.9 us (6%)
  starting transfers between devices  28.4 us (5%)
  between operations  14.8 us (3%)
    all_to_all x2, blocking collectives, on_device(): lax.all_to_all(near_modes, 'gy', split_axis=3, concat_axis=4, tiled=True)  104 us
    all_to_all x3, waiting for transfers between devices, on_device(): lax.all_to_all(back_rows, 'gy', split_axis=4, concat_axis=3, tiled=True)  64.3 us
    dot_general x3, matrix products, on_device(): jnp.einsum('lrcky,rkx->lcyx', own_modes, table_ix, preferred_element_type...  50.4 us
    unnamed x37, local copies, waits for them, and re-layouts  50 us
    all_to_all x1, waiting for transfers between devices, on_device(): lax.all_to_all(near_modes, 'gy', split_axis=3, concat_axis=4, tiled=True)  42.9 us
    dot_general x3, matrix products, on_device(): jnp.einsum('lcyx,co->loyx', current, point_weight, preferred_element_type...  39.6 us
    convert_element_type x3, local copies, waits for them, and re-layouts, on_device(): back_rows = jnp.einsum('klqcm,qmry->lrcky', mixed, table_iy, preferred_el...  27.5 us
    all_to_all x3, local copies, waits for them, and re-layouts, on_device(): lax.all_to_all(back_rows, 'gy', split_axis=4, concat_axis=3, tiled=True)  25.5 us
  transfers between devices with their start and end apart: 8, of which 8 were waited for; matrix products, arithmetic and copies ran while one was open for 8% of the time, Pallas kernels for 0%

commit v1 on v0

--- a/solution.py
+++ b/solution.py
@@ -119,7 +119,12 @@
         near_modes = jnp.einsum(
             "lcyx,rxk->lrcky", current, table_fx, preferred_element_type=jnp.float32
         ).astype(jnp.bfloat16)
-        all_rows = lax.all_to_all(near_modes, "gy", split_axis=3, concat_axis=4, tiled=True)
+        all_rows = jnp.concatenate(
+            lax.all_to_all(
+                jnp.stack(jnp.split(near_modes, lax.axis_size("gy"), axis=3)), "gy", 0, 0
+            ),
+            axis=4,
+        )
         table_fy = forward_y(every_row, total_rows, ymode_count)
         spectrum = jnp.einsum(
             "lrcky,ryqm->klqcm", all_rows, table_fy, preferred_element_type=jnp.float32

time: 571 us -> 643 us (1.13)
  local copies, waits for them, and re-layouts: 129 us -> 198 us
    another operation x3 -> x36, local copies, waits for them, and re-layouts: 7.97 us -> 75.1 us  [the longest x30 61.5 us: on_device(): jnp.stack(jnp.split(near_modes, lax.axis_size('gy'), axis=3))]
    unnamed x37 -> x120, local copies, waits for them, and re-layouts: 50 us -> 67.1 us
    convert_element_type x3 -> x0, local copies, waits for them, and re-layouts: 9.67 us -> none  [on_device(): near_modes = jnp.einsum('lcyx,rxk->lrcky', current, table_fx, preferred_e...]
  transfers between devices with their start and end apart: 8 -> 8, of which waited for: 8 -> 8; matrix products, arithmetic and copies ran while one was open for 8% -> 7% of each run, Pallas kernels for 0% -> 0%
where the time goes in v1:
time: 643 us; the launch traced here: 636 us
  local copies, waits for them, and re-layouts  198 us (31%)
  waiting for transfers between devices  138 us (21%)
  matrix products  120 us (19%)
  blocking collectives  104 us (16%)
  other arithmetic  32.4 us (5%)
  starting transfers between devices  28.3 us (4%)
  between operations  15.2 us (2%)
    all_to_all x2, blocking collectives, on_device(): lax.all_to_all(jnp.stack(jnp.split(near_modes, lax.axis_size('gy'), axis=...  104 us
    unnamed x120, local copies, waits for them, and re-layouts  67.1 us
    all_to_all x3, waiting for transfers between devices, on_device(): lax.all_to_all(back_rows, 'gy', split_axis=4, concat_axis=3, tiled=True)  65.4 us
    another operation x30, local copies, waits for them, and re-layouts, on_device(): jnp.stack(jnp.split(near_modes, lax.axis_size('gy'), axis=3))  61.5 us
    dot_general x3, matrix products, on_device(): jnp.einsum('lrcky,rkx->lcyx', own_modes, table_ix, preferred_element_type...  53.1 us
    all_to_all x1, waiting for transfers between devices, on_device(): lax.all_to_all(jnp.stack(jnp.split(near_modes, lax.axis_size('gy'), axis=...  42.9 us
    dot_general x3, matrix products, on_device(): jnp.einsum('lcyx,co->loyx', current, point_weight, preferred_element_type...  39.7 us
    convert_element_type x3, local copies, waits for them, and re-layouts, on_device(): back_rows = jnp.einsum('klqcm,qmry->lrcky', mixed, table_iy, preferred_el...  27.5 us
  transfers between devices with their start and end apart: 8, of which 8 were waited for; matrix products, arithmetic and copies ran while one was open for 7% of the time, Pallas kernels for 0%

profile of v1, /device:TPU:1, one launch (start us, length us, event | category | flops | bytes accessed | tf_op | source)
XLA Modules:
  0.0 635.8 jit_solution(3613972186984817604)
XLA Ops:
  10.2 4.6 fusion.67
  14.8 5.1 slice_bitcast_fusion.16
  22.3 2.3 copy.138
  24.6 2.3 copy.139
  41.1 6.9 %all-to-all-start = ((bf16[8,1,2,32,16,96]{5,4,3,2,1,0:T(8,128)(2,1)}), bf16[8,1,2,32,16,96]{5,4,3,2,1,0:T(8,128)(2,1)S(1)}, u32[]{:S(2)}, u32[]{:S(2)}) async-start(bf16[8,1,2,32,16,96]{5,4,3,2,1,0:T(8,128)(2,1)} %constant_dynamic-update-slice_fusion), calls=%async_computation | async-start | bytes 4194304 | tf_op jit(solution)/shard_map/all_to_all | solution.py:123
  52.5 42.9 %all-to-all-done = bf16[8,1,2,32,16,96]{5,4,3,2,1,0:T(8,128)(2,1)S(1)} async-done(((bf16[8,1,2,32,16,96]{5,4,3,2,1,0:T(8,128)(2,1)}), bf16[8,1,2,32,16,96]{5,4,3,2,1,0:T(8,128)(2,1)S(1)}, u32[]{:S(2)}, u32[]{:S(2)}) %all-to-all-start) | async-done | bytes 1572896 | tf_op jit(solution)/shard_map/all_to_all | solution.py:123
  96.8 2.9 copy.289
  99.7 2.7 reshape.721
  104.6 5.1 fusion.31
  110.4 9.2 %copy.147 = bf16[1,2,32,16,768]{2,3,1,0,4:T(8,128)(2,1)} copy(bf16[1,2,32,16,768]{4,2,3,1,0:T(8,128)(2,1)S(1)} %fusion.58) | data formatting | bytes 3145728 | tf_op jit(solution)/shard_map/convert_element_type | solution.py:136
  119.5 9.5 %reshape.774 = bf16[8,2,49152]{2,1,0:T(2,128)(2,1)} reshape(bf16[768,1,2,16,32]{4,3,2,1,0:T(8,128)(2,1)} %bitcast.410) | data formatting | bytes 3145728
  129.1 4.8 all-to-all-start.1
  136.2 16.5 %fusion.47 = f32[32,96,1024]{2,0,1:T(8,128)} fusion(bf16[32,96,1024]{2,1,0:T(8,128)(2,1)} %bitcast.425, bf16[32,32]{1,0:T(8,128)(2,1)S(1)} %copy-done), kind=kOutput, calls=%fused_computation.70 | convolution fusion | flops 201326592 | bytes 18876416 | tf_op jit(solution)/shard_map/lcyx,co->loyx/dot_general | solution.py:141
  152.7 17.6 %all-to-all-done.1 = bf16[8,2,49152]{2,1,0:T(2,128)(2,1)S(1)} async-done(((bf16[8,2,49152]{2,1,0:T(2,128)(2,1)}), bf16[8,2,49152]{2,1,0:T(2,128)(2,1)S(1)}, u32[]{:S(2)}, u32[]{:S(2)}) %all-to-all-start.1) | async-done | bytes 1572896 | tf_op jit(solution)/shard_map/all_to_all | solution.py:137
  170.2 5.4 reshape.775
  175.6 8.5 %copy.148 = bf16[1,2,32,16,8,96]{5,3,4,2,1,0:T(8,128)(2,1)S(1)} copy(bf16[1,2,32,16,8,96]{2,3,1,5,4,0:T(8,128)(2,1)} %bitcast.411) | data formatting | bytes 3145728 | tf_op jit(solution)/shard_map/all_to_all | solution.py:137
  184.2 17.8 %fusion.7 = bf16[1,32,96,1024]{3,2,1,0:T(8,128)(2,1)S(1)} fusion(f32[32,96,1024]{2,0,1:T(8,128)} %fusion.47, bf16[1,32,96,1024]{3,2,1,0:T(8,128)(2,1)} %param.9, f32[32]{0:T(128)S(1)} %copy-done.44, bf16[2,32,128,96]{3,2,1,0:T(8,128)(2,1)S(1)} %bitcast.429, bf16[1,128,1024]{2,1,0:T(8,128)(2,1)S(1)} %get-tuple-element.188, ...), kind=kOutput, calls=%fused_computation.23 | convolution fusion | flops 1651769344 | bytes 27263104 | tf_op jit(solution)/shard_map/lrcky,rkx->lcyx/dot_general | solution.py:138
  204.6 5.1 slice_bitcast_fusion.8
  231.4 51.7 %all_to_all.60 = bf16[8,1,2,32,16,96]{5,4,3,2,1,0:T(8,128)(2,1)S(1)} all-to-all(bf16[8,1,2,32,16,96]{5,4,3,2,1,0:T(8,128)(2,1)} %constant_dynamic-update-slice_fusion.8), channel_id=1, replica_groups=mesh['lev'=4,'gy'=8] {'gy'}, dimensions={0} | all-to-all | bytes 3145728 | tf_op jit(solution)/shard_map/all_to_all | solution.py:123
  284.5 2.7 reshape.738
  289.2 5.2 fusion.33
  295.1 9.2 %copy.163 = bf16[1,2,32,16,768]{2,3,1,0,4:T(8,128)(2,1)} copy(bf16[1,2,32,16,768]{4,2,3,1,0:T(8,128)(2,1)S(1)} %fusion.59) | data formatting | bytes 3145728 | tf_op jit(solution)/shard_map/convert_element_type | solution.py:136
  304.3 9.5 %reshape.776 = bf16[8,2,49152]{2,1,0:T(2,128)(2,1)} reshape(bf16[768,1,2,16,32]{4,3,2,1,0:T(8,128)(2,1)} %bitcast.412) | data formatting | bytes 3145728
  313.8 4.3 all-to-all-start.3
  318.0 11.6 %fusion.45 = f32[96,1024,32]{1,2,0:T(8,128)} fusion(bf16[32,96,1024]{2,1,0:T(8,128)(2,1)} %bitcast.427, bf16[32,32]{1,0:T(8,128)(2,1)S(1)} %copy-done), kind=kOutput, calls=%fused_computation.68 | convolution fusion | flops 201326592 | bytes 18876416 | tf_op jit(solution)/shard_map/lcyx,co->loyx/dot_general | solution.py:141
  329.6 24.2 %all-to-all-done.3 = bf16[8,2,49152]{2,1,0:T(2,128)(2,1)S(1)} async-done(((bf16[8,2,49152]{2,1,0:T(2,128)(2,1)}), bf16[8,2,49152]{2,1,0:T(2,128)(2,1)S(1)}, u32[]{:S(2)}, u32[]{:S(2)}) %all-to-all-start.3) | async-done | bytes 1572896 | tf_op jit(solution)/shard_map/all_to_all | solution.py:137
  353.9 5.4 reshape.777
  359.2 8.6 %copy.164 = bf16[1,2,32,16,8,96]{5,3,4,2,1,0:T(8,128)(2,1)S(1)} copy(bf16[1,2,32,16,8,96]{2,3,1,5,4,0:T(8,128)(2,1)} %bitcast.413) | data formatting | bytes 3145728 | tf_op jit(solution)/shard_map/all_to_all | solution.py:137
  367.8 17.7 %fusion.15 = bf16[1,32,96,1024]{3,2,1,0:T(8,128)(2,1)S(1)} fusion(f32[96,1024,32]{1,2,0:T(8,128)} %fusion.45, bf16[1,32,96,1024]{3,2,1,0:T(8,128)(2,1)} %param.9, f32[32]{0:T(128)S(1)} %copy-done.44, bf16[2,32,128,96]{3,2,1,0:T(8,128)(2,1)S(1)} %bitcast.430, bf16[1,128,1024]{2,1,0:T(8,128)(2,1)S(1)} %copy-done.36, bf16[1,128,1024]{2,1,0:T(8,128)(2,1)S(1)} %copy-done.39), kind=kOutput, calls=%fused_computation.31 | convolution fusion | flops 1651769344 | bytes 27263104 | tf_op jit(solution)/shard_map/lrcky,rkx->lcyx/dot_general | solution.py:138
  388.3 5.1 slice_bitcast_fusion
  414.8 52.2 %all_to_all.61 = bf16[8,1,2,32,16,96]{5,4,3,2,1,0:T(8,128)(2,1)S(1)} all-to-all(bf16[8,1,2,32,16,96]{5,4,3,2,1,0:T(8,128)(2,1)} %constant_dynamic-update-slice_fusion.16), channel_id=1, replica_groups=mesh['lev'=4,'gy'=8] {'gy'}, dimensions={0} | all-to-all | bytes 3145728 | tf_op jit(solution)/shard_map/all_to_all | solution.py:123
  468.4 2.7 reshape.753
  473.1 5.2 fusion.35
  479.0 9.2 %copy.179 = bf16[1,2,32,16,768]{2,3,1,0,4:T(8,128)(2,1)} copy(bf16[1,2,32,16,768]{4,2,3,1,0:T(8,128)(2,1)S(1)} %fusion.60) | data formatting | bytes 3145728 | tf_op jit(solution)/shard_map/convert_element_type | solution.py:136
  488.1 9.5 %reshape.778 = bf16[8,2,49152]{2,1,0:T(2,128)(2,1)} reshape(bf16[768,1,2,16,32]{4,3,2,1,0:T(8,128)(2,1)} %bitcast.414) | data formatting | bytes 3145728
  497.6 4.4 all-to-all-start.5
  502.7 11.6 %fusion.43 = f32[96,1024,32]{1,2,0:T(8,128)} fusion(bf16[32,96,1024]{2,1,0:T(8,128)(2,1)} %bitcast.426, bf16[32,32]{1,0:T(8,128)(2,1)S(1)} %copy-done), kind=kOutput, calls=%fused_computation.66 | convolution fusion | flops 201326592 | bytes 18876416 | tf_op jit(solution)/shard_map/lcyx,co->loyx/dot_general | solution.py:141
  514.3 23.6 %all-to-all-done.5 = bf16[8,2,49152]{2,1,0:T(2,128)(2,1)S(1)} async-done(((bf16[8,2,49152]{2,1,0:T(2,128)(2,1)}), bf16[8,2,49152]{2,1,0:T(2,128)(2,1)S(1)}, u32[]{:S(2)}, u32[]{:S(2)}) %all-to-all-start.5) | async-done | bytes 1572896 | tf_op jit(solution)/shard_map/all_to_all | solution.py:137
  537.9 5.8 reshape.779
  543.7 8.6 %copy.180 = bf16[1,2,32,16,8,96]{5,3,4,2,1,0:T(8,128)(2,1)S(1)} copy(bf16[1,2,32,16,8,96]{2,3,1,5,4,0:T(8,128)(2,1)} %bitcast.415) | data formatting | bytes 3145728 | tf_op jit(solution)/shard_map/all_to_all | solution.py:137
  552.3 17.6 %fusion.22 = f32[1,32,96,1024]{3,2,1,0:T(8,128)S(1)} fusion(f32[96,1024,32]{1,2,0:T(8,128)} %fusion.43, bf16[1,32,96,1024]{3,2,1,0:T(8,128)(2,1)} %param.9, f32[32]{0:T(128)S(1)} %copy-done.44, bf16[2,32,128,96]{3,2,1,0:T(8,128)(2,1)S(1)} %bitcast.428, bf16[1,128,1024]{2,1,0:T(8,128)(2,1)S(1)} %copy-done.37, bf16[1,128,1024]{2,1,0:T(8,128)(2,1)S(1)} %copy-done.40), kind=kOutput, calls=%fused_computation.38 | convolution fusion | flops 1648623616 | bytes 33554560 | tf_op jit(solution)/shard_map/lrcky,rkx->lcyx/dot_general | solution.py:138
  569.9 11.3 %fusion.23 = f32[96,1024,4]{1,2,0:T(4,128)S(1)} fusion(f32[32,96,1024]{2,1,0:T(8,128)S(1)} %bitcast.421, bf16[4,32]{1,0:T(4,128)(2,1)S(1)} %copy-done.41), kind=kOutput, calls=%fused_computation.45 | convolution fusion | flops 150994944 | bytes 14156032 | tf_op jit(solution)/shard_map/lcyx,fc->flyx/dot_general | solution.py:146
  583.7 20.7 %all-gather.2.cloned.1.call-done = f32[4,96,1024]{2,1,0:T(8,128)} async-done(((f32[1,96,1024]{2,1,0:T(8,128)}), f32[4,96,1024]{2,1,0:T(8,128)}) %all-gather.2.cloned.1.call-update) | async-done | bytes 1572880 | tf_op jit(solution)/shard_map/all_gather | solution.py:12
  604.4 4.7 while.14
  609.2 4.0 collective-permute-start
  614.0 4.4 collective-permute-done.1
  618.9 3.8 collective-permute-start.2
  622.9 4.4 collective-permute-done.2
  (186 shorter events, 97.4 us)
Async XLA Ops:
  7.2 129.0 %copy-start = (bf16[32,32]{1,0:T(8,128)(2,1)S(1)}, bf16[32,32]{1,0:T(8,128)(2,1)}, u32[]{:S(2)}) copy-start(bf16[32,32]{1,0:T(8,128)(2,1)} %param.11) | copy-start | bytes 6148
  34.4 3.1 copy-start.12
  34.4 3.8 copy-start.9
  34.5 4.5 copy-start.6
  41.1 54.3 %all-to-all-start = ((bf16[8,1,2,32,16,96]{5,4,3,2,1,0:T(8,128)(2,1)}), bf16[8,1,2,32,16,96]{5,4,3,2,1,0:T(8,128)(2,1)S(1)}, u32[]{:S(2)}, u32[]{:S(2)}) async-start(bf16[8,1,2,32,16,96]{5,4,3,2,1,0:T(8,128)(2,1)} %constant_dynamic-update-slice_fusion), calls=%async_computation | async-start | bytes 4194304 | tf_op jit(solution)/shard_map/all_to_all | solution.py:123
  50.6 51.7 %copy-start.24 = (bf16[1,768,2,128]{3,1,0,2:T(8,128)(2,1)}, bf16[1,768,2,128]{3,1,0,2:T(8,128)(2,1)S(1)}, u32[]{:S(2)}) copy-start(bf16[1,768,2,128]{3,1,0,2:T(8,128)(2,1)S(1)} %get-tuple-element.178) | copy-start | bytes 1179652
  52.5 57.3 %copy-start.18 = (bf16[1,128,2,768]{3,1,0,2:T(8,128)(2,1)}, bf16[1,128,2,768]{3,1,0,2:T(8,128)(2,1)S(1)}, u32[]{:S(2)}) copy-start(bf16[1,128,2,768]{3,1,0,2:T(8,128)(2,1)S(1)} %get-tuple-element.176) | copy-start | bytes 1179652
  52.5 57.3 %copy-start.21 = (bf16[1,128,2,768]{3,1,0,2:T(8,128)(2,1)}, bf16[1,128,2,768]{3,1,0,2:T(8,128)(2,1)S(1)}, u32[]{:S(2)}) copy-start(bf16[1,128,2,768]{3,1,0,2:T(8,128)(2,1)S(1)} %get-tuple-element.177) | copy-start | bytes 1179652
  129.1 41.2 %all-to-all-start.1 = ((bf16[8,2,49152]{2,1,0:T(2,128)(2,1)}), bf16[8,2,49152]{2,1,0:T(2,128)(2,1)S(1)}, u32[]{:S(2)}, u32[]{:S(2)}) async-start(bf16[8,2,49152]{2,1,0:T(2,128)(2,1)} %reshape.774), calls=%async_computation.1 | async-start | bytes 3145728 | tf_op jit(solution)/shard_map/all_to_all | solution.py:137
  136.1 48.0 %copy-start.35 = (bf16[1,128,1024]{2,1,0:T(8,128)(2,1)}, bf16[1,128,1024]{2,1,0:T(8,128)(2,1)S(1)}, u32[]{:S(2)}) copy-start(bf16[1,128,1024]{2,1,0:T(8,128)(2,1)S(1)} %get-tuple-element.188) | copy-start | bytes 786436
  136.1 48.0 %copy-start.38 = (bf16[1,128,1024]{2,1,0:T(8,128)(2,1)}, bf16[1,128,1024]{2,1,0:T(8,128)(2,1)S(1)}, u32[]{:S(2)}) copy-start(bf16[1,128,1024]{2,1,0:T(8,128)(2,1)S(1)} %get-tuple-element.189) | copy-start | bytes 786436
  175.6 8.5 %copy-start.44 = (f32[32]{0:T(128)S(1)}, f32[32]{0:T(128)}, u32[]{:S(2)}) copy-start(f32[32]{0:T(128)} %param.12) | copy-start | bytes 388
  184.1 17.8 %copy-start.30 = (bf16[1,1024,128]{2,1,0:T(8,128)(2,1)S(1)}, bf16[1,1024,128]{2,1,0:T(8,128)(2,1)}, u32[]{:S(2)}) copy-start(bf16[1,1024,128]{2,1,0:T(8,128)(2,1)} %copy-done.29) | copy-start | bytes 786436
  184.2 17.8 %copy-start.33 = (bf16[1,1024,128]{2,1,0:T(8,128)(2,1)S(1)}, bf16[1,1024,128]{2,1,0:T(8,128)(2,1)}, u32[]{:S(2)}) copy-start(bf16[1,1024,128]{2,1,0:T(8,128)(2,1)} %copy-done.32) | copy-start | bytes 786436
  201.9 2.7 copy-start.4
  224.3 2.8 copy-start.16
  224.3 3.6 copy-start.13
  224.3 4.3 copy-start.10
  224.3 5.0 copy-start.7
  284.5 2.7 copy-start.25
  284.5 2.7 copy-start.27
  289.2 5.3 copy-start.19
  289.2 5.3 copy-start.22
  313.8 40.1 %all-to-all-start.3 = ((bf16[8,2,49152]{2,1,0:T(2,128)(2,1)}), bf16[8,2,49152]{2,1,0:T(2,128)(2,1)S(1)}, u32[]{:S(2)}, u32[]{:S(2)}) async-start(bf16[8,2,49152]{2,1,0:T(2,128)(2,1)} %reshape.776), calls=%async_computation.3 | async-start | bytes 3145728 | tf_op jit(solution)/shard_map/all_to_all | solution.py:137
  359.2 8.6 %copy-start.36 = (bf16[1,128,1024]{2,1,0:T(8,128)(2,1)S(1)}, bf16[1,128,1024]{2,1,0:T(8,128)(2,1)}, u32[]{:S(2)}) copy-start(bf16[1,128,1024]{2,1,0:T(8,128)(2,1)} %copy-done.35) | copy-start | bytes 786436
  359.2 8.6 %copy-start.39 = (bf16[1,128,1024]{2,1,0:T(8,128)(2,1)S(1)}, bf16[1,128,1024]{2,1,0:T(8,128)(2,1)}, u32[]{:S(2)}) copy-start(bf16[1,128,1024]{2,1,0:T(8,128)(2,1)} %copy-done.38) | copy-start | bytes 786436
  367.8 17.8 %copy-start.31 = (bf16[1,1024,128]{2,1,0:T(8,128)(2,1)S(1)}, bf16[1,1024,128]{2,1,0:T(8,128)(2,1)}, u32[]{:S(2)}) copy-start(bf16[1,1024,128]{2,1,0:T(8,128)(2,1)} %copy-done.29) | copy-start | bytes 786436
  367.8 17.8 %copy-start.34 = (bf16[1,1024,128]{2,1,0:T(8,128)(2,1)S(1)}, bf16[1,1024,128]{2,1,0:T(8,128)(2,1)}, u32[]{:S(2)}) copy-start(bf16[1,1024,128]{2,1,0:T(8,128)(2,1)} %copy-done.32) | copy-start | bytes 786436
  385.6 2.7 copy-start.3
  407.9 3.3 copy-start.14
  407.9 4.0 copy-start.11
  407.9 4.7 copy-start.8
  468.4 2.7 copy-start.26
  468.4 2.7 copy-start.28
  473.1 5.3 copy-start.20
  473.1 5.3 copy-start.23
  497.6 4.5 copy-start.43
  497.6 40.2 %all-to-all-start.5 = ((bf16[8,2,49152]{2,1,0:T(2,128)(2,1)}), bf16[8,2,49152]{2,1,0:T(2,128)(2,1)S(1)}, u32[]{:S(2)}, u32[]{:S(2)}) async-start(bf16[8,2,49152]{2,1,0:T(2,128)(2,1)} %reshape.778), calls=%async_computation.5 | async-start | bytes 3145728 | tf_op jit(solution)/shard_map/all_to_all | solution.py:137
  502.0 102.4 %all-gather.2.cloned.1.call-start = ((), (), s32[]{:S(2)}) async-start(), calls=%async_computation.6 | async-start | bytes 1966080 | tf_op jit(solution)/shard_map/all_gather | solution.py:12
  543.7 8.6 %copy-start.37 = (bf16[1,128,1024]{2,1,0:T(8,128)(2,1)S(1)}, bf16[1,128,1024]{2,1,0:T(8,128)(2,1)}, u32[]{:S(2)}) copy-start(bf16[1,128,1024]{2,1,0:T(8,128)(2,1)} %copy-done.35) | copy-start | bytes 786436
  543.7 8.6 %copy-start.40 = (bf16[1,128,1024]{2,1,0:T(8,128)(2,1)S(1)}, bf16[1,128,1024]{2,1,0:T(8,128)(2,1)}, u32[]{:S(2)}) copy-start(bf16[1,128,1024]{2,1,0:T(8,128)(2,1)} %copy-done.38) | copy-start | bytes 786436
  552.2 17.6 %copy-start.41 = (bf16[4,32]{1,0:T(4,128)(2,1)S(1)}, bf16[4,32]{1,0:T(4,128)(2,1)}, u32[]{:S(2)}) copy-start(bf16[4,32]{1,0:T(4,128)(2,1)} %param.13) | copy-start | bytes 772
  569.9 11.3 %copy-start.1 = (f32[1,32,96,1024]{3,2,1,0:T(8,128)}, f32[1,32,96,1024]{3,2,1,0:T(8,128)S(1)}, u32[]{:S(2)}) copy-start(f32[1,32,96,1024]{3,2,1,0:T(8,128)S(1)} %fusion.22) | copy-start | bytes 37748740
  604.4 4.7 copy-start.5
  609.2 9.4 %copy-start.42 = (f32[96]{0:T(128)S(1)}, f32[96]{0:T(128)}, u32[]{:S(2)}) copy-start(f32[96]{0:T(128)} %param.14) | copy-start | bytes 1156
  609.2 4.8 collective-permute-start
  613.2 5.2 collective-permute-start.1
  618.9 8.5 %collective-permute-start.2 = (f32[96,1024]{1,0:T(8,128)S(1)}, f32[96,1024]{1,0:T(8,128)S(1)}, u32[]{:S(2)}, u32[]{:S(2)}) collective-permute-start(f32[96,1024]{1,0:T(8,128)S(1)} %get-tuple-element.135), channel_id=1, source_target_pairs={{0,8},{8,16},{16,24},{1,9},{9,17},{17,25},{2,10},{10,18},{18,26},{... | collective-permute-start | bytes 1179656 | tf_op jit(solution)/shard_map/ppermute | solution.py:26
  (5 other events, 7.8 us)
Sparse Core Ops, SparseCore 0:
  583.9 20.5 all-gather.1
